TPU v7x, 256 devices: a whole 4x4x8 slice. The times are simulated.
256 devices in a mesh: ctx: 16 (over y, x), exp: 8 (over z), dp: 2 (over core).
Axes of the slice: x: 4, y: 4, z: 8, core: 2. Of those that a mesh axis runs over, the one named last changes fastest.
Arguments:
- residual: bfloat16 [2048, 4096], P('ctx', ('exp', 'dp')), may hold values from -6 to 6
- ssm_values: bfloat16 [2048, 4096], P('ctx', ('exp', 'dp')), may hold values from -6 to 6
- ssm_keys: bfloat16 [2048, 64], P('ctx'), may hold values from -6 to 6
- ssm_queries: bfloat16 [2048, 64], P('ctx'), may hold values from -0.015625 to 0.015625
- log_decay: float32 [2048, 64], P('ctx', ('exp', 'dp')), may hold values from -1 to 0, as said below
- expert_ids: int32 [2048, 2], P('ctx'), may hold values from 0 to 7, all different within a row; in each aligned block of 128 rows (0 to 127, 128 to 255, ...) at most 40 rows name the same one
- gate_probs: float32 [2048, 2], P('ctx'), may hold values from 0.2 to 1
- norm_gain: float32 [4096], P(('exp', 'dp')), may hold values from 0.5 to 1.5
- w_gate: bfloat16 [8, 4096, 8192], P('exp', None, ('ctx', 'dp')), may hold values from -0.09375 to 0.09375
- w_up: bfloat16 [8, 4096, 8192], P('exp', None, ('ctx', 'dp')), may hold values from -0.09375 to 0.09375
- w_down: bfloat16 [8, 4096, 8192], P('exp', None, ('ctx', 'dp')), may hold values from -0.0625 to 0.0625
- out_grad: bfloat16 [2048, 4096], P('ctx', ('exp', 'dp')), may hold values from -6 to 6
Outputs:
- grad_residual: bfloat16 [2048, 4096], P('ctx', ('exp', 'dp'))
- grad_values: bfloat16 [2048, 4096], P('ctx', ('exp', 'dp'))
- grad_keys: float32 [2048, 64], P('ctx')
- grad_queries: float32 [2048, 64], P('ctx')
- grad_decay: float32 [2048, 64], P('ctx', ('exp', 'dp'))
- grad_probs: float32 [2048, 2], P('ctx')
- grad_gain: float32 [4096], P(('exp', 'dp'))
- w_gate_grad: bfloat16 [8, 4096, 8192], P('exp', None, ('ctx', 'dp'))
- w_up_grad: bfloat16 [8, 4096, 8192], P('exp', None, ('ctx', 'dp'))
- w_down_grad: bfloat16 [8, 4096, 8192], P('exp', None, ('ctx', 'dp'))
Inputs may be any that keep to these rules, and one draw needn't show every extreme that they name: `expert_ids`: each token names two different experts; among the 128 tokens of one index of ctx (aligned blocks) no expert is named more than 40 times, a bound that some block reaches. `log_decay`: negative everywhere.
All inputs are finite; a program needn't handle non-finite values.
Results may differ from a plain program's by a relative error of at most 0.028.
Values may be sent and summed in bfloat16 or wider, within the bound.
No kernel may reach another device: no remote copies, remote signals or barrier semaphores. Data moves between devices by JAX's collectives and lax.ppermute only.
A program may use at most 128 MiB of HBM per device.

v0:
```python
import jax
import jax.numpy as jnp
from jax import lax
from jax.sharding import PartitionSpec as P

HIGH = lax.Precision.HIGHEST
EPS = 1e-05


def entering(x, axis, join, neutral):
    place = lax.axis_index(axis)
    gathered = jax.tree.map(
        lambda a, kind: lax.all_gather(a.astype(kind), axis), x, (jnp.bfloat16, jnp.bfloat16)
    )
    state = jax.tree.map(lambda a, e: jnp.zeros_like(a) + jnp.asarray(e, a.dtype), x, neutral)

    def entering_one(step, state):
        return join(
            state,
            jax.tree.map(
                lambda a, own: lax.dynamic_index_in_dim(a, step, 0, False).astype(own.dtype),
                gathered,
                x,
            ),
        )

    return lax.fori_loop(0, place, entering_one, state)


def carried_in(x, axis, join, neutral):
    count = lax.axis_size(axis)
    place = lax.axis_index(axis)
    ahead = count - 1 - place
    gathered = jax.tree.map(
        lambda a, kind: lax.all_gather(a.astype(kind), axis),
        x,
        jax.tree.map(lambda a: jnp.bfloat16 if a.dtype == jnp.float32 else a.dtype, x),
    )
    state = jax.tree.map(lambda a, e: jnp.zeros_like(a) + jnp.asarray(e, a.dtype), x, neutral)

    def carried_one(step, state):
        source = count - 1 - step
        return join(
            state,
            jax.tree.map(
                lambda a, own: lax.dynamic_index_in_dim(a, source, 0, False).astype(own.dtype),
                gathered,
                x,
            ),
        )

    return lax.fori_loop(0, ahead, carried_one, state)


def block_state(values, key_rows, log_decay):
    cumulative = jnp.cumsum(log_decay, axis=0)
    total_log = cumulative[-1]
    tail_decay = jnp.exp(total_log[None, :] - cumulative)
    weighted = tail_decay[:, :, None] * values
    state_local = jnp.einsum("shp,sn->hpn", weighted, key_rows, precision=HIGH)
    return (jnp.exp(total_log), state_local)


def block_output(values, key_rows, queries, log_decay, state_in):
    cumulative = jnp.cumsum(log_decay, axis=0)
    length = values.shape[0]
    row_index = lax.broadcasted_iota(jnp.int32, (length, length), 0)
    col_index = lax.broadcasted_iota(jnp.int32, (length, length), 1)
    causal = (row_index >= col_index)[None]
    cum_heads = cumulative.T
    log_gap = jnp.where(causal, cum_heads[:, :, None] - cum_heads[:, None, :], 0.0)
    decay_mat = jnp.where(causal, jnp.exp(log_gap), 0.0)
    scores = jnp.dot(queries, key_rows.T, precision=HIGH)
    inner_part = jnp.einsum("hts,shp->thp", decay_mat * scores[None], values, precision=HIGH)
    carried = jnp.einsum("tn,hpn->thp", queries, state_in, precision=HIGH)
    return inner_part + jnp.exp(cumulative)[:, :, None] * carried


def silu_parts(gate_act):
    sigmoid_val = jax.nn.sigmoid(gate_act)
    return (gate_act * sigmoid_val, sigmoid_val * (1.0 + gate_act * (1.0 - sigmoid_val)))


def route_slots(token_ids, expert_count):
    owners = token_ids.reshape(-1)
    onehot = (owners[:, None] == jnp.arange(expert_count, dtype=jnp.int32)[None, :]).astype(
        jnp.int32
    )
    rank_before = jnp.cumsum(onehot, axis=0) - onehot
    return (owners, jnp.sum(rank_before * onehot, axis=1))


def combine_states(earlier_part, later_part):
    return (
        earlier_part[0] * later_part[0],
        later_part[0][:, None, None] * earlier_part[1] + later_part[1],
    )


def arrange_rows(gathered, ctx_count, dp_count):
    capacity = gathered.shape[1]
    exp_count = gathered.shape[2]
    feat = gathered.shape[3]
    shaped = gathered.reshape(ctx_count, dp_count, capacity, exp_count, feat)
    return shaped.transpose(0, 2, 3, 1, 4).reshape(
        ctx_count * capacity, exp_count * dp_count * feat
    )


def arrange_sums(full_term, ctx_count, dp_count, exp_count, capacity):
    feat = full_term.shape[1] // (exp_count * dp_count)
    shaped = full_term.reshape(ctx_count, capacity, exp_count, dp_count, feat)
    return shaped.transpose(0, 3, 1, 2, 4).reshape(
        ctx_count * dp_count * capacity, exp_count * feat
    )


def per_device(
    residual,
    ssm_values,
    ssm_keys,
    ssm_queries,
    log_decay,
    expert_ids,
    gate_probs,
    norm_gain,
    w_gate,
    w_up,
    w_down,
    out_grad,
):
    tokens = residual.shape[0]
    feat = residual.shape[1]
    heads_here = log_decay.shape[1]
    head_size = feat // heads_here
    model_width = w_gate.shape[1]
    ctx_count = lax.axis_size("ctx")
    exp_count = lax.axis_size("exp")
    dp_count = lax.axis_size("dp")
    expert_count = w_gate.shape[0] * exp_count
    capacity = 5 * tokens // (2 * expert_count)
    block_vals = ssm_values.astype(jnp.float32).reshape(tokens, heads_here, head_size)
    block_keys = ssm_keys.astype(jnp.float32)
    block_queries = ssm_queries.astype(jnp.float32)
    (decay_total, state_local), state_pull = jax.vjp(block_state, block_vals, block_keys, log_decay)
    neutral = (jnp.ones_like(decay_total), jnp.zeros_like(state_local))
    state_in = entering((decay_total, state_local), "ctx", combine_states, neutral)[1]
    mixer_out, output_pull = jax.vjp(
        block_output, block_vals, block_keys, block_queries, log_decay, state_in
    )
    hidden = (residual.astype(jnp.float32) + mixer_out.reshape(tokens, feat)).astype(jnp.bfloat16)
    hidden_f = hidden.astype(jnp.float32)
    square_sum = lax.psum(jnp.sum(hidden_f * hidden_f, axis=1), ("exp", "dp"))
    inv_rms = lax.rsqrt(square_sum / model_width + EPS)[:, None]
    normed = (hidden_f * inv_rms * norm_gain[None, :]).astype(jnp.bfloat16)
    owners, slot_index = route_slots(expert_ids, expert_count)
    pair_rows = jnp.repeat(normed, 2, axis=0)
    dout_rows = jnp.repeat(out_grad, 2, axis=0)
    pair_prob = gate_probs.reshape(-1)
    pair_cot = (pair_prob[:, None] * dout_rows.astype(jnp.float32)).astype(jnp.bfloat16)
    empty = jnp.zeros((expert_count, capacity, feat), jnp.bfloat16)
    send_rows = empty.at[owners, slot_index].set(pair_rows).reshape(expert_count, capacity, 1, feat)
    got_rows = lax.all_to_all(send_rows, "exp", split_axis=0, concat_axis=2, tiled=True)
    all_rows = lax.all_gather(got_rows, ("ctx", "dp"), axis=0, tiled=True)
    rows_flat = arrange_rows(all_rows, ctx_count, dp_count)
    act_gate = jnp.dot(rows_flat, w_gate[0], preferred_element_type=jnp.float32)
    act_up = jnp.dot(rows_flat, w_up[0], preferred_element_type=jnp.float32)
    swish_val, swish_slope = silu_parts(act_gate)
    hidden_act = (swish_val * act_up).astype(jnp.bfloat16)
    full_out = lax.dot_general(
        hidden_act, w_down[0], (((1,), (1,)), ((), ())), preferred_element_type=jnp.float32
    )
    out_total = lax.psum_scatter(
        arrange_sums(full_out, ctx_count, dp_count, exp_count, capacity).astype(jnp.bfloat16),
        ("ctx", "dp"),
        scatter_dimension=0,
        tiled=True,
    )
    expert_out = out_total.reshape(1, capacity, exp_count, feat)
    back_out = lax.all_to_all(expert_out, "exp", split_axis=2, concat_axis=0, tiled=True).reshape(
        expert_count, capacity, feat
    )
    out_pairs = back_out[owners, slot_index]
    probs_part = jnp.einsum(
        "kd,kd->k", out_pairs, dout_rows, preferred_element_type=jnp.float32
    ).reshape(tokens, 2)
    grad_probs = lax.psum(probs_part, ("exp", "dp"))
    send_cot = empty.at[owners, slot_index].set(pair_cot).reshape(expert_count, capacity, 1, feat)
    got_cot = lax.all_to_all(send_cot, "exp", split_axis=0, concat_axis=2, tiled=True)
    all_cot = lax.all_gather(got_cot, ("ctx", "dp"), axis=0, tiled=True)
    cot_flat = arrange_rows(all_cot, ctx_count, dp_count)
    grad_act = jnp.dot(cot_flat, w_down[0], preferred_element_type=jnp.float32)
    grad_gate = (grad_act * act_up * swish_slope).astype(jnp.bfloat16)
    grad_up = (grad_act * swish_val).astype(jnp.bfloat16)
    full_back = lax.dot_general(
        grad_gate, w_gate[0], (((1,), (1,)), ((), ())), preferred_element_type=jnp.float32
    ) + lax.dot_general(
        grad_up, w_up[0], (((1,), (1,)), ((), ())), preferred_element_type=jnp.float32
    )
    back_total = lax.psum_scatter(
        arrange_sums(full_back, ctx_count, dp_count, exp_count, capacity).astype(jnp.bfloat16),
        ("ctx", "dp"),
        scatter_dimension=0,
        tiled=True,
    )
    pair_back = back_total.reshape(1, capacity, exp_count, feat)
    back_in = lax.all_to_all(pair_back, "exp", split_axis=2, concat_axis=0, tiled=True).reshape(
        expert_count, capacity, feat
    )
    grad_normed = (
        back_in[owners, slot_index].astype(jnp.float32).reshape(tokens, 2, feat).sum(axis=1)
    )
    w_gate_grad = jnp.dot(rows_flat.T, grad_gate, preferred_element_type=jnp.float32).astype(
        jnp.bfloat16
    )[None]
    w_up_grad = jnp.dot(rows_flat.T, grad_up, preferred_element_type=jnp.float32).astype(
        jnp.bfloat16
    )[None]
    w_down_grad = jnp.dot(cot_flat.T, hidden_act, preferred_element_type=jnp.float32).astype(
        jnp.bfloat16
    )[None]
    scaled = grad_normed * norm_gain[None, :]
    inner_sum = lax.psum(jnp.sum(hidden_f * scaled, axis=1), ("exp", "dp"))
    projection = (inner_sum / model_width)[:, None]
    grad_hidden = (
        out_grad.astype(jnp.float32) + inv_rms * scaled - hidden_f * inv_rms**3 * projection
    )
    gain_part = jnp.sum(grad_normed * hidden_f * inv_rms, axis=0)
    grad_gain = lax.psum(gain_part, "ctx")
    grad_mixer = grad_hidden.reshape(tokens, heads_here, head_size)
    vals_first, keys_first, queries_part, decay_first, carry_cot = output_pull(grad_mixer)
    grad_state = carried_in((decay_total, carry_cot), "ctx", combine_states, neutral)[1]
    grad_total = jnp.sum(grad_state * state_in, axis=(1, 2))
    vals_second, keys_second, decay_second = state_pull((grad_total, grad_state))
    grad_keys, grad_queries = (
        lax.psum((keys_first + keys_second).astype(jnp.bfloat16), ("exp", "dp")).astype(
            jnp.float32
        ),
        lax.psum(queries_part.astype(jnp.bfloat16), ("exp", "dp")).astype(jnp.float32),
    )
    grad_residual = grad_hidden.astype(jnp.bfloat16)
    grad_values = (vals_first + vals_second).reshape(tokens, feat).astype(jnp.bfloat16)
    grad_decay = decay_first + decay_second
    return (
        grad_residual,
        grad_values,
        grad_keys,
        grad_queries,
        grad_decay,
        grad_probs,
        grad_gain,
        w_gate_grad,
        w_up_grad,
        w_down_grad,
    )


def solution(mesh):
    return jax.shard_map(
        per_device,
        mesh=mesh,
        in_specs=(
            P("ctx", ("exp", "dp")),
            P("ctx", ("exp", "dp")),
            P("ctx", None),
            P("ctx", None),
            P("ctx", ("exp", "dp")),
            P("ctx", None),
            P("ctx", None),
            P(("exp", "dp")),
            P("exp", None, ("ctx", "dp")),
            P("exp", None, ("ctx", "dp")),
            P("exp", None, ("ctx", "dp")),
            P("ctx", ("exp", "dp")),
        ),
        out_specs=(
            P("ctx", ("exp", "dp")),
            P("ctx", ("exp", "dp")),
            P("ctx", None),
            P("ctx", None),
            P("ctx", ("exp", "dp")),
            P("ctx", None),
            P(("exp", "dp")),
            P("exp", None, ("ctx", "dp")),
            P("exp", None, ("ctx", "dp")),
            P("exp", None, ("ctx", "dp")),
        ),
        check_vma=False,
    )
```

profile of v0, /device:TPU:2, one launch (start us, length us, event | category | flops | bytes accessed | tf_op | source)
XLA Modules:
  0.0 650.5 jit_solution(5369685150378966095)
XLA Ops:
  11.6 13.2 %scatter_fusion = bf16[8,40,256]{2,1,0:T(8,128)(2,1)S(1)} fusion(bf16[8,40,256]{2,1,0:T(8,128)(2,1)S(1)} %broadcast_in_dim.73.clone.1, s32[256]{0:T(256)S(1)} %bitcast.193, bf16[256,256]{1,0:T(8,128)(2,1)S(1)} %fusion.19), kind=kCustom, calls=%fused_computation.2 | custom fusion | bytes 395264 | tf_op jit(solution)/shard_map/scatter | solution.py:188
  24.9 18.0 %all_to_all.66 = bf16[8,40,1,256]{3,1,2,0:T(8,128)(2,1)S(1)} all-to-all(bf16[8,40,1,256]{3,1,2,0:T(8,128)(2,1)S(1)} %bitcast.200), channel_id=1, replica_groups=mesh['ctx'=16,'exp'=8,'dp'=2] {'exp'}, dimensions={0} | all-to-all | bytes 327680 | tf_op jit(solution)/shard_map/all_to_all | solution.py:189
  44.6 20.7 %all-gather.4 = bf16[16,1,4]{2,1,0:T(2,128)(2,1)S(1)} all-gather(bf16[1,1,4]{2,1,0:T(2,128)(2,1)S(1)} %get-tuple-element.299), channel_id=1, replica_groups=mesh['ctx'=16,'exp'=8,'dp'=2] {'ctx'}, dimensions={0}, use_global_device_ids=true | all-gather | bytes 136 | tf_op jit(solution)/shard_map/all_gather | solution.py:13
  65.4 1.0 copy.152
  67.0 27.6 %all-gather = bf16[64,64,64]{2,1,0:T(8,128)(2,1)} all-gather(bf16[4,64,64]{2,1,0:T(8,128)(2,1)S(1)} %convolution_convert_fusion.4), channel_id=2, replica_groups=mesh['ctx'=16,'exp'=8,'dp'=2] {'ctx'}, dimensions={0}, use_global_device_ids=true | all-gather | bytes 557056 | tf_op jit(solution)/shard_map/all_gather | solution.py:13
  94.8 1.0 while.26
  94.9 0.9 convert_add_fusion.4
  96.7 23.5 %psum.42 = f32[128]{0:T(128)S(1)} all-reduce(f32[128]{0:T(128)S(1)} %get-tuple-element.291), channel_id=1, replica_groups=mesh['ctx'=16,'exp'=8,'dp'=2] {'exp','dp'}, use_global_device_ids=true, to_apply=%region_4.5 | all-reduce | flops 128 | bytes 1024 | tf_op jit(solution)/shard_map/psum | solution.py:153
  121.1 13.2 %scatter_fusion.1 = bf16[8,40,256]{2,1,0:T(8,128)(2,1)S(1)} fusion(bf16[8,40,256]{2,1,0:T(8,128)(2,1)S(1)} %broadcast_in_dim.73.clone, s32[256]{0:T(256)S(1)} %bitcast.194, bf16[256,256]{1,0:T(8,128)(2,1)S(1)} %reshape.273), kind=kCustom, calls=%fused_computation.3 | custom fusion | bytes 395264 | tf_op jit(solution)/shard_map/scatter | solution.py:162
  134.3 12.5 %all_to_all.67 = bf16[8,40,1,256]{3,1,2,0:T(8,128)(2,1)S(1)} all-to-all(bf16[8,40,1,256]{3,1,2,0:T(8,128)(2,1)S(1)} %bitcast.199), channel_id=1, replica_groups=mesh['ctx'=16,'exp'=8,'dp'=2] {'exp'}, dimensions={0} | all-to-all | bytes 327680 | tf_op jit(solution)/shard_map/all_to_all | solution.py:163
  148.1 13.0 %copy.164 = bf16[16,40,8,2,256]{4,3,2,1,0:T(2,128)(2,1)} copy(bf16[16,40,8,2,256]{4,2,1,3,0:T(8,128)(2,1)} %bitcast.203) | data formatting | bytes 10485760 | tf_op jit(solution)/shard_map/transpose | solution.py:105
  161.1 9.6 %reshape.236 = bf16[640,4096]{1,0:T(8,128)(2,1)} reshape(bf16[16,40,8,2,256]{4,3,2,1,0:T(2,128)(2,1)} %copy.164) | data formatting | bytes 10485760 | tf_op jit(solution)/shard_map/reshape | solution.py:105
  170.7 35.8 %all-gather.10.cloned.1.call-done = bf16[32,40,8,1,256]{4,2,3,1,0:T(8,128)(2,1)} async-done(((bf16[1,40,8,1,256]{4,2,3,1,0:T(8,128)(2,1)}), bf16[32,40,8,1,256]{4,2,3,1,0:T(8,128)(2,1)}) %all-gather.10.cloned.1.call-update) | async-done | bytes 5242896 | tf_op jit(solution)/shard_map/all_gather | solution.py:164
  206.6 13.0 %copy.167 = bf16[16,40,8,2,256]{4,3,2,1,0:T(2,128)(2,1)} copy(bf16[16,40,8,2,256]{4,2,1,3,0:T(8,128)(2,1)} %bitcast.204) | data formatting | bytes 10485760 | tf_op jit(solution)/shard_map/transpose | solution.py:105
  219.6 9.6 %reshape.240 = bf16[640,4096]{1,0:T(8,128)(2,1)} reshape(bf16[16,40,8,2,256]{4,3,2,1,0:T(2,128)(2,1)} %copy.167) | data formatting | bytes 10485760 | tf_op jit(solution)/shard_map/reshape | solution.py:105
  229.2 4.2 fusion.10
  233.9 1.5 fusion.5
  235.5 2.4 multiply_convert_fusion
  238.0 1.6 convert_bitcast_fusion
  239.6 2.3 copy.176
  241.9 4.6 copy.191
  247.0 1.1 copy-done.4
  248.2 1.6 fusion.3
  249.8 3.8 add_convert_fusion
  253.6 9.6 %convert_element_type.165 = bf16[16,40,8,2,256]{4,3,2,1,0:T(2,128)(2,1)} reshape(bf16[640,4096]{1,0:T(8,128)(2,1)} %add_convert_fusion) | data formatting | bytes 10485760 | tf_op jit(solution)/shard_map/convert_element_type | solution.py:201
  263.2 3.6 copy.168
  266.8 4.5 copy.189
  271.3 1.0 copy-done.10
  272.3 5.9 fusion.2
  278.2 60.3 %reduce-scatter.5.cloned.1.call-done = bf16[40,2048]{1,0:T(8,128)(2,1)} async-done(((bf16[1280,2048]{1,0:T(8,128)(2,1)}), bf16[40,2048]{1,0:T(8,128)(2,1)}) %reduce-scatter.5.cloned.1.call-update) | async-done | bytes 163856 | tf_op jit(solution)/shard_map/reduce_scatter | solution.py:173
  338.5 0.9 copy.192
  340.1 7.0 %all-to-all-start.3 = ((bf16[1,40,8,256]{3,1,0,2:T(8,128)(2,1)}), bf16[1,40,8,256]{3,1,0,2:T(8,128)(2,1)S(1)}, u32[]{:S(2)}, u32[]{:S(2)}) async-start(bf16[1,40,8,256]{3,1,0,2:T(8,128)(2,1)} %copy.177), calls=%async_computation.5 | async-start | bytes 327680 | tf_op jit(solution)/shard_map/all_to_all | solution.py:180
  347.2 5.7 fusion
  352.9 81.2 %reduce-scatter.3.cloned.1.call-done = bf16[40,2048]{1,0:T(8,128)(2,1)} async-done(((bf16[1280,2048]{1,0:T(8,128)(2,1)}), bf16[40,2048]{1,0:T(8,128)(2,1)}) %reduce-scatter.3.cloned.1.call-update) | async-done | bytes 163856 | tf_op jit(solution)/shard_map/reduce_scatter | solution.py:200
  434.1 0.9 copy.190
  435.8 7.2 %all-to-all-start.2 = ((bf16[1,40,8,256]{3,1,0,2:T(8,128)(2,1)}), bf16[1,40,8,256]{3,1,0,2:T(8,128)(2,1)S(1)}, u32[]{:S(2)}, u32[]{:S(2)}) async-start(bf16[1,40,8,256]{3,1,0,2:T(8,128)(2,1)} %copy.169), calls=%async_computation.3 | async-start | bytes 327680 | tf_op jit(solution)/shard_map/all_to_all | solution.py:207
  443.0 5.7 fusion.1
  448.7 1.7 gather_fusion.1
  450.6 1.7 all-to-all-done.2
  452.4 1.7 gather_fusion
  454.6 46.5 %all-reduce.1 = (f32[128]{0:T(128)S(1)}, f32[128,2]{1,0:T(8,128)S(1)}) all-reduce(f32[128]{0:T(128)S(1)} %get-tuple-element.264, f32[128,2]{1,0:T(8,128)S(1)} %reshape.247), channel_id=1, replica_groups=mesh['ctx'=16,'exp'=8,'dp'=2] {'exp','dp'}, use_global_device_ids=true, to_apply=%region_13.14 | all-reduce | flops 384 | bytes 3072 | tf_op jit(solution)/shard_map/psum | solution.py:223
  502.6 25.1 %all-gather.3 = bf16[64,64,64]{2,1,0:T(8,128)(2,1)} all-gather(bf16[4,64,64]{2,1,0:T(8,128)(2,1)S(1)} %convolution_convert_fusion.3), channel_id=5, replica_groups=mesh['ctx'=16,'exp'=8,'dp'=2] {'ctx'}, dimensions={0}, use_global_device_ids=true | all-gather | bytes 557056 | tf_op jit(solution)/shard_map/all_gather | solution.py:35
  527.7 22.9 %while.27 = (s32[]{:T(128)}, f32[4,64,64]{2,1,0:T(8,128)S(1)}, s32[]{:T(128)}, bf16[16,4]{1,0:T(8,128)(2,1)}, bf16[16,4,64,64]{3,2,1,0:T(8,128)(2,1)}, /*index=5*/s32[]{:T(128)}, s32[]{:T(128)}, s32[]{:T(128)}, s32[]{:T(128)}) while((s32[]{:T(128)}, f32[4,64,64]{2,1,0:T(8,128)S(1)}, s32[]{:T(128)}, bf16[16,4]{1,0:T(8,128)(2,1)}, ...), condition=%wide.region_15.16_spmd, body=%wide.region_14.15_spmd.sunk | while | flops 49162 | bytes 164035 | solution.py:52
  549.7 0.9 convert_add_fusion.5
  550.9 39.5 %psum.47 = f32[256]{0:T(256)} all-reduce(f32[256]{0:T(256)S(1)} %get-tuple-element.263), channel_id=1, replica_groups=mesh['ctx'=16,'exp'=8,'dp'=2] {'ctx'}, use_global_device_ids=true, to_apply=%region_30.31 | all-reduce | flops 256 | bytes 2048 | tf_op jit(solution)/shard_map/psum | solution.py:229
  593.7 45.7 %all-reduce.2 = (bf16[128,64]{0,1:T(8,128)(2,1)S(1)}, bf16[128,64]{0,1:T(8,128)(2,1)S(1)}) all-reduce(bf16[128,64]{0,1:T(8,128)(2,1)S(1)} %fusion.16, bf16[128,64]{0,1:T(8,128)(2,1)S(1)} %fusion.17), channel_id=1, replica_groups=mesh['ctx'=16,'exp'=8,'dp'=2] {'exp','dp'}, use_global_device_ids=true, to_apply=%region_17.18 | all-reduce | flops 16384 | bytes 65536 | tf_op jit(solution)/shard_map/psum | solution.py:236
  640.8 1.1 reduce_window_sum.47
  641.9 1.1 reduce_window_sum.48
  (155 shorter events, 42.0 us)
Async XLA Ops:
  7.2 222.0 %copy-start = (bf16[1,4096,256]{2,1,0:T(8,128)(2,1)S(1)}, bf16[1,4096,256]{2,1,0:T(8,128)(2,1)}, u32[]{:S(2)}) copy-start(bf16[1,4096,256]{2,1,0:T(8,128)(2,1)} %param.26) | copy-start | bytes 6291460
  7.2 59.6 %copy-start.13 = (bf16[128,64]{0,1:T(8,128)(2,1)S(1)}, bf16[128,64]{0,1:T(8,128)(2,1)}, u32[]{:S(2)}) copy-start(bf16[128,64]{0,1:T(8,128)(2,1)} %param.18) | copy-start | bytes 49156
  7.2 87.4 %copy-start.12 = (bf16[128,64]{0,1:T(8,128)(2,1)S(1)}, bf16[128,64]{0,1:T(8,128)(2,1)}, u32[]{:S(2)}) copy-start(bf16[128,64]{0,1:T(8,128)(2,1)} %param.19) | copy-start | bytes 49156
  7.2 89.4 %copy-start.16 = (bf16[128,256]{1,0:T(8,128)(2,1)S(1)}, bf16[128,256]{1,0:T(8,128)(2,1)}, u32[]{:S(2)}) copy-start(bf16[128,256]{1,0:T(8,128)(2,1)} %param.16) | copy-start | bytes 196612
  7.2 113.6 %copy-start.17 = (f32[256]{0:T(256)S(1)}, f32[256]{0:T(256)}, u32[]{:S(2)}) copy-start(f32[256]{0:T(256)} %param.23) | copy-start | bytes 3076
  7.2 140.9 %all-gather.8.cloned.1.call-start = ((), (), s32[]{:S(2)}) async-start(), calls=%async_computation.8 | async-start | bytes 5406720 | tf_op jit(solution)/shard_map/all_gather | solution.py:190
  43.6 163.0 %all-gather.10.cloned.1.call-start = ((), (), s32[]{:S(2)}) async-start(), calls=%async_computation.9 | async-start | bytes 5406720 | tf_op jit(solution)/shard_map/all_gather | solution.py:164
  66.4 67.9 %copy-start.19 = (f32[4,128]{1,0:T(4,128)}, f32[4,128]{1,0:T(4,128)S(1)}, u32[]{:S(2)}) copy-start(f32[4,128]{1,0:T(4,128)S(1)} %copy.150) | copy-start | bytes 6148
  94.8 39.5 %copy-start.14 = (f32[128,128]{1,0:T(8,128)}, f32[128,128]{1,0:T(8,128)S(1)}, u32[]{:S(2)}) copy-start(f32[128,128]{1,0:T(8,128)S(1)} %fusion.65) | copy-start | bytes 196612
  95.8 38.5 %copy-start.18 = (bf16[16,4]{1,0:T(8,128)(2,1)}, bf16[16,4]{1,0:T(8,128)(2,1)S(1)}, u32[]{:S(2)}) copy-start(bf16[16,4]{1,0:T(8,128)(2,1)S(1)} %get-tuple-element.437) | copy-start | bytes 388
  147.5 191.0 %reduce-scatter.5.cloned.1.call-start = ((), (), s32[]{:S(2)}) async-start(), calls=%async_computation.7 | async-start | bytes 5406720 | tf_op jit(solution)/shard_map/reduce_scatter | solution.py:173
  229.2 4.2 copy-start.2
  229.2 4.7 copy-start.3
  233.9 1.6 copy-start.5
  238.0 3.9 copy-start.9
  246.6 1.6 copy-start.4
  246.6 187.5 %reduce-scatter.3.cloned.1.call-start = ((), (), s32[]{:S(2)}) async-start(), calls=%async_computation.6 | async-start | bytes 5406720 | tf_op jit(solution)/shard_map/reduce_scatter | solution.py:200
  248.2 1.6 copy-start.6
  248.2 1.6 copy-start.7
  271.3 1.0 copy-start.10
  340.1 95.7 %all-to-all-start.3 = ((bf16[1,40,8,256]{3,1,0,2:T(8,128)(2,1)}), bf16[1,40,8,256]{3,1,0,2:T(8,128)(2,1)S(1)}, u32[]{:S(2)}, u32[]{:S(2)}) async-start(bf16[1,40,8,256]{3,1,0,2:T(8,128)(2,1)} %copy.177), calls=%async_computation.5 | async-start | bytes 327680 | tf_op jit(solution)/shard_map/all_to_all | solution.py:180
  347.2 95.8 %copy-start.8 = (bf16[640,256]{1,0:T(8,128)(2,1)S(1)}, bf16[640,256]{1,0:T(8,128)(2,1)}, u32[]{:S(2)}) copy-start(bf16[640,256]{1,0:T(8,128)(2,1)} %get-tuple-element.297) | copy-start | bytes 983044
  435.8 16.6 %all-to-all-start.2 = ((bf16[1,40,8,256]{3,1,0,2:T(8,128)(2,1)}), bf16[1,40,8,256]{3,1,0,2:T(8,128)(2,1)S(1)}, u32[]{:S(2)}, u32[]{:S(2)}) async-start(bf16[1,40,8,256]{3,1,0,2:T(8,128)(2,1)} %copy.169), calls=%async_computation.3 | async-start | bytes 327680 | tf_op jit(solution)/shard_map/all_to_all | solution.py:207
  443.0 58.1 %copy-start.11 = (bf16[128,256]{1,0:T(8,128)(2,1)S(1)}, bf16[128,256]{1,0:T(8,128)(2,1)}, u32[]{:S(2)}) copy-start(bf16[128,256]{1,0:T(8,128)(2,1)} %param.27) | copy-start | bytes 196612
  443.0 58.1 %copy-start.21 = (f32[128]{0:T(128)S(1)}, f32[128]{0:T(128)}, u32[]{:S(2)}) copy-start(f32[128]{0:T(128)} %get-tuple-element.300) | copy-start | bytes 1540
  448.7 142.3 %copy-start.15 = (f32[128,128]{1,0:T(8,128)S(1)}, f32[128,128]{1,0:T(8,128)}, u32[]{:S(2)}) copy-start(f32[128,128]{1,0:T(8,128)} %copy-done.14) | copy-start | bytes 196612
  448.7 142.3 %copy-start.20 = (f32[4,128]{1,0:T(4,128)S(1)}, f32[4,128]{1,0:T(4,128)}, u32[]{:S(2)}) copy-start(f32[4,128]{1,0:T(4,128)} %copy-done.19) | copy-start | bytes 6148
  452.4 191.4 %copy-start.1 = (bf16[1,4096,256]{2,1,0:T(8,128)(2,1)S(1)}, bf16[1,4096,256]{2,1,0:T(8,128)(2,1)}, u32[]{:S(2)}) copy-start(bf16[1,4096,256]{2,1,0:T(8,128)(2,1)} %param.26) | copy-start | bytes 6291460
Sparse Core Ops, SparseCore 0:
  43.7 49.1 all-gather.7
  147.6 58.8 all-gather.9
  246.7 91.7 reduce-scatter.4
  342.4 91.7 reduce-scatter.2
where the time goes:
time: 657 us; the launch traced here: 650 us
  blocking collectives  259 us (39%)
  waiting for transfers between devices  179 us (27%)
  local copies, waits for them, and re-layouts  116 us (18%)
  matrix products  35.9 us (5%)
  other arithmetic  30.4 us (5%)
  starting transfers between devices  15.3 us (2%)
  between operations  14.5 us (2%)
    reduce_scatter x1, waiting for transfers between devices, per_device(): lax.psum_scatter(arrange_sums(full_back, ctx_count, dp_count, exp_count,...  81.2 us
    reduce_scatter x1, waiting for transfers between devices, per_device(): lax.psum_scatter(arrange_sums(full_out, ctx_count, dp_count, exp_count, c...  60.3 us
    all_gather x2, blocking collectives, entering(): lax.all_gather(a.astype(kind), axis)  48.3 us
    psum x1, blocking collectives, per_device(): inner_sum = lax.psum(jnp.sum(hidden_f * scaled, axis=1), ('exp', 'dp'))  46.5 us
    psum x1, blocking collectives, per_device(): lax.psum((keys_first + keys_second).astype(jnp.bfloat16), ('exp', 'dp'))  45.7 us
    psum x1, blocking collectives, per_device(): grad_gain = lax.psum(gain_part, 'ctx')  39.5 us
    all_gather x1, waiting for transfers between devices, per_device(): all_rows = lax.all_gather(got_rows, ('ctx', 'dp'), axis=0, tiled=True)  35.8 us
    transpose x2, local copies, waits for them, and re-layouts, arrange_rows(): shaped.transpose(0, 2, 3, 1, 4)  26 us
  transfers between devices with their start and end apart: 6, of which 4 were waited for; matrix products, arithmetic and copies ran while one was open for 13% of the time, Pallas kernels for 0%

commit v1 on v0

--- a/solution.py
+++ b/solution.py
@@ -161,7 +161,10 @@
     empty = jnp.zeros((expert_count, capacity, feat), jnp.bfloat16)
     send_rows = empty.at[owners, slot_index].set(pair_rows).reshape(expert_count, capacity, 1, feat)
     got_rows = lax.all_to_all(send_rows, "exp", split_axis=0, concat_axis=2, tiled=True)
-    all_rows = lax.all_gather(got_rows, ("ctx", "dp"), axis=0, tiled=True)
+    all_rows = jnp.concatenate(
+        lax.all_to_all(jnp.stack([got_rows] * lax.axis_size(("ctx", "dp"))), ("ctx", "dp"), 0, 0),
+        axis=0,
+    )
     rows_flat = arrange_rows(all_rows, ctx_count, dp_count)
     act_gate = jnp.dot(rows_flat, w_gate[0], preferred_element_type=jnp.float32)
     act_up = jnp.dot(rows_flat, w_up[0], preferred_element_type=jnp.float32)

time: 657 us -> 701 us (1.067)
  blocking collectives: 259 us -> 338 us
  waiting for transfers between devices: 179 us -> 137 us
    all_to_all x0 -> x1, blocking collectives: none -> 79.4 us  [per_device(): lax.all_to_all(jnp.stack([got_rows] * lax.axis_size(('ctx', 'dp'))), ('ct...]
    all_gather x1 -> x0, waiting for transfers between devices: 35.8 us -> none  [per_device(): all_rows = lax.all_gather(got_rows, ('ctx', 'dp'), axis=0, tiled=True)]
    unnamed x55 -> x53, local copies, waits for them, and re-layouts: 19.4 us -> 19 us
  transfers between devices with their start and end apart: 6 -> 5, of which waited for: 4 -> 3; matrix products, arithmetic and copies ran while one was open for 13% -> 13% of each run, Pallas kernels for 0% -> 0%
where the time goes in v1:
time: 701 us; the launch traced here: 694 us
  blocking collectives  338 us (48%)
  waiting for transfers between devices  137 us (20%)
  local copies, waits for them, and re-layouts  116 us (17%)
  matrix products  42.4 us (6%)
  other arithmetic  30.4 us (4%)
  starting transfers between devices  14.6 us (2%)
  between operations  14.5 us (2%)
    reduce_scatter x1, waiting for transfers between devices, per_device(): lax.psum_scatter(arrange_sums(full_back, ctx_count, dp_count, exp_count,...  81.4 us
    all_to_all x1, blocking collectives, per_device(): lax.all_to_all(jnp.stack([got_rows] * lax.axis_size(('ctx', 'dp'))), ('ct...  79.4 us
    reduce_scatter x1, waiting for transfers between devices, per_device(): lax.psum_scatter(arrange_sums(full_out, ctx_count, dp_count, exp_count, c...  54.2 us
    all_gather x2, blocking collectives, entering(): lax.all_gather(a.astype(kind), axis)  48.3 us
    psum x1, blocking collectives, per_device(): inner_sum = lax.psum(jnp.sum(hidden_f * scaled, axis=1), ('exp', 'dp'))  46.5 us
    psum x1, blocking collectives, per_device(): lax.psum((keys_first + keys_second).astype(jnp.bfloat16), ('exp', 'dp'))  45.7 us
    psum x1, blocking collectives, per_device(): grad_gain = lax.psum(gain_part, 'ctx')  39.5 us
    transpose x2, local copies, waits for them, and re-layouts, arrange_rows(): shaped.transpose(0, 2, 3, 1, 4)  26 us
  transfers between devices with their start and end apart: 5, of which 3 were waited for; matrix products, arithmetic and copies ran while one was open for 13% of the time, Pallas kernels for 0%

profile of v1, /device:TPU:2, one launch (start us, length us, event | category | flops | bytes accessed | tf_op | source)
XLA Modules:
  0.0 693.6 jit_solution(12553914316293552880)
XLA Ops:
  11.6 13.2 %scatter_fusion = bf16[8,40,256]{2,1,0:T(8,128)(2,1)S(1)} fusion(bf16[8,40,256]{2,1,0:T(8,128)(2,1)S(1)} %broadcast_in_dim.73.clone.1, s32[256]{0:T(256)S(1)} %bitcast.195, bf16[256,256]{1,0:T(8,128)(2,1)S(1)} %fusion.19), kind=kCustom, calls=%fused_computation.2 | custom fusion | bytes 395264 | tf_op jit(solution)/shard_map/scatter | solution.py:191
  24.9 18.0 %all_to_all.68 = bf16[8,40,1,256]{3,1,2,0:T(8,128)(2,1)S(1)} all-to-all(bf16[8,40,1,256]{3,1,2,0:T(8,128)(2,1)S(1)} %bitcast.203), channel_id=1, replica_groups=mesh['ctx'=16,'exp'=8,'dp'=2] {'exp'}, dimensions={0} | all-to-all | bytes 327680 | tf_op jit(solution)/shard_map/all_to_all | solution.py:192
  44.6 20.7 %all-gather.3 = bf16[16,1,4]{2,1,0:T(2,128)(2,1)S(1)} all-gather(bf16[1,1,4]{2,1,0:T(2,128)(2,1)S(1)} %get-tuple-element.299), channel_id=1, replica_groups=mesh['ctx'=16,'exp'=8,'dp'=2] {'ctx'}, dimensions={0}, use_global_device_ids=true | all-gather | bytes 136 | tf_op jit(solution)/shard_map/all_gather | solution.py:13
  65.4 1.0 copy.154
  67.0 27.6 %all-gather = bf16[64,64,64]{2,1,0:T(8,128)(2,1)} all-gather(bf16[4,64,64]{2,1,0:T(8,128)(2,1)S(1)} %convolution_convert_fusion.4), channel_id=2, replica_groups=mesh['ctx'=16,'exp'=8,'dp'=2] {'ctx'}, dimensions={0}, use_global_device_ids=true | all-gather | bytes 557056 | tf_op jit(solution)/shard_map/all_gather | solution.py:13
  94.8 1.0 while.26
  94.9 0.9 convert_add_fusion.4
  96.7 23.5 %psum.42 = f32[128]{0:T(128)S(1)} all-reduce(f32[128]{0:T(128)S(1)} %get-tuple-element.291), channel_id=1, replica_groups=mesh['ctx'=16,'exp'=8,'dp'=2] {'exp','dp'}, use_global_device_ids=true, to_apply=%region_4.5 | all-reduce | flops 128 | bytes 1024 | tf_op jit(solution)/shard_map/psum | solution.py:153
  121.1 13.2 %scatter_fusion.1 = bf16[8,40,256]{2,1,0:T(8,128)(2,1)S(1)} fusion(bf16[8,40,256]{2,1,0:T(8,128)(2,1)S(1)} %broadcast_in_dim.73.clone, s32[256]{0:T(256)S(1)} %bitcast.196, bf16[256,256]{1,0:T(8,128)(2,1)S(1)} %reshape.274), kind=kCustom, calls=%fused_computation.3 | custom fusion | bytes 395264 | tf_op jit(solution)/shard_map/scatter | solution.py:162
  134.3 12.5 %all_to_all.69 = bf16[8,40,1,256]{3,1,2,0:T(8,128)(2,1)S(1)} all-to-all(bf16[8,40,1,256]{3,1,2,0:T(8,128)(2,1)S(1)} %bitcast.202), channel_id=1, replica_groups=mesh['ctx'=16,'exp'=8,'dp'=2] {'exp'}, dimensions={0} | all-to-all | bytes 327680 | tf_op jit(solution)/shard_map/all_to_all | solution.py:163
  147.4 79.4 %all_to_all.70 = bf16[32,1,40,8,256]{4,3,2,1,0:T(8,128)(2,1)} all-to-all(bf16[32,1,40,8,256]{4,3,2,1,0:T(8,128)(2,1)S(1)} %stack.5), channel_id=1, replica_groups=mesh['ctx'=16,'exp'=8,'dp'=2] {'ctx','dp'}, dimensions={0} | all-to-all | bytes 10485760 | tf_op jit(solution)/shard_map/all_to_all | solution.py:165
  226.8 13.0 %copy.169 = bf16[16,40,8,2,256]{4,3,2,1,0:T(2,128)(2,1)} copy(bf16[16,40,8,2,256]{4,2,1,3,0:T(8,128)(2,1)} %bitcast.199) | data formatting | bytes 10485760 | tf_op jit(solution)/shard_map/transpose | solution.py:105
  239.8 9.6 %reshape.241 = bf16[640,4096]{1,0:T(8,128)(2,1)} reshape(bf16[16,40,8,2,256]{4,3,2,1,0:T(2,128)(2,1)} %copy.169) | data formatting | bytes 10485760 | tf_op jit(solution)/shard_map/reshape | solution.py:105
  249.5 5.5 fusion.5
  255.0 13.0 %copy.166 = bf16[16,40,8,2,256]{4,3,2,1,0:T(2,128)(2,1)} copy(bf16[16,40,8,2,256]{4,2,1,3,0:T(8,128)(2,1)} %bitcast.206) | data formatting | bytes 10485760 | tf_op jit(solution)/shard_map/transpose | solution.py:105
  268.0 9.8 %reshape.238 = bf16[640,4096]{1,0:T(8,128)(2,1)} reshape(bf16[16,40,8,2,256]{4,3,2,1,0:T(2,128)(2,1)} %copy.166) | data formatting | bytes 10485760 | tf_op jit(solution)/shard_map/reshape | solution.py:105
  277.9 4.2 fusion.10
  282.0 5.0 multiply_convert_fusion
  287.0 1.6 convert_bitcast_fusion
  288.6 2.3 copy.178
  290.9 4.6 copy.193
  295.8 1.3 copy-done.2
  297.2 1.6 fusion.3
  298.8 3.8 add_convert_fusion
  302.6 9.7 %convert_element_type.165 = bf16[16,40,8,2,256]{4,3,2,1,0:T(2,128)(2,1)} reshape(bf16[640,4096]{1,0:T(8,128)(2,1)} %add_convert_fusion) | data formatting | bytes 10485760 | tf_op jit(solution)/shard_map/convert_element_type | solution.py:204
  312.2 3.6 copy.170
  315.9 4.5 copy.191
  320.4 1.0 copy-done.8
  321.4 5.9 fusion.2
  327.2 54.2 %reduce-scatter.5.cloned.1.call-done = bf16[40,2048]{1,0:T(8,128)(2,1)} async-done(((bf16[1280,2048]{1,0:T(8,128)(2,1)}), bf16[40,2048]{1,0:T(8,128)(2,1)}) %reduce-scatter.5.cloned.1.call-update) | async-done | bytes 163856 | tf_op jit(solution)/shard_map/reduce_scatter | solution.py:176
  381.4 0.9 copy.194
  383.1 7.0 %all-to-all-start.4 = ((bf16[1,40,8,256]{3,1,0,2:T(8,128)(2,1)}), bf16[1,40,8,256]{3,1,0,2:T(8,128)(2,1)S(1)}, u32[]{:S(2)}, u32[]{:S(2)}) async-start(bf16[1,40,8,256]{3,1,0,2:T(8,128)(2,1)} %copy.179), calls=%async_computation.6 | async-start | bytes 327680 | tf_op jit(solution)/shard_map/all_to_all | solution.py:183
  390.1 5.7 fusion
  395.8 81.4 %reduce-scatter.3.cloned.1.call-done = bf16[40,2048]{1,0:T(8,128)(2,1)} async-done(((bf16[1280,2048]{1,0:T(8,128)(2,1)}), bf16[40,2048]{1,0:T(8,128)(2,1)}) %reduce-scatter.3.cloned.1.call-update) | async-done | bytes 163856 | tf_op jit(solution)/shard_map/reduce_scatter | solution.py:203
  477.2 0.9 copy.192
  478.8 7.3 %all-to-all-start.3 = ((bf16[1,40,8,256]{3,1,0,2:T(8,128)(2,1)}), bf16[1,40,8,256]{3,1,0,2:T(8,128)(2,1)S(1)}, u32[]{:S(2)}, u32[]{:S(2)}) async-start(bf16[1,40,8,256]{3,1,0,2:T(8,128)(2,1)} %copy.171), calls=%async_computation.4 | async-start | bytes 327680 | tf_op jit(solution)/shard_map/all_to_all | solution.py:210
  486.1 5.7 fusion.1
  491.8 1.7 gather_fusion.1
  493.8 1.7 all-to-all-done.3
  495.5 1.7 gather_fusion
  497.8 46.5 %all-reduce.1 = (f32[128]{0:T(128)S(1)}, f32[128,2]{1,0:T(8,128)S(1)}) all-reduce(f32[128]{0:T(128)S(1)} %get-tuple-element.264, f32[128,2]{1,0:T(8,128)S(1)} %reshape.248), channel_id=1, replica_groups=mesh['ctx'=16,'exp'=8,'dp'=2] {'exp','dp'}, use_global_device_ids=true, to_apply=%region_13.14 | all-reduce | flops 384 | bytes 3072 | tf_op jit(solution)/shard_map/psum | solution.py:226
  545.7 25.0 %all-gather.2 = bf16[64,64,64]{2,1,0:T(8,128)(2,1)} all-gather(bf16[4,64,64]{2,1,0:T(8,128)(2,1)S(1)} %convolution_convert_fusion.3), channel_id=4, replica_groups=mesh['ctx'=16,'exp'=8,'dp'=2] {'ctx'}, dimensions={0}, use_global_device_ids=true | all-gather | bytes 557056 | tf_op jit(solution)/shard_map/all_gather | solution.py:35
  570.8 22.9 %while.27 = (s32[]{:T(128)}, f32[4,64,64]{2,1,0:T(8,128)S(1)}, s32[]{:T(128)}, bf16[16,4]{1,0:T(8,128)(2,1)}, bf16[16,4,64,64]{3,2,1,0:T(8,128)(2,1)}, /*index=5*/s32[]{:T(128)}, s32[]{:T(128)}, s32[]{:T(128)}, s32[]{:T(128)}) while((s32[]{:T(128)}, f32[4,64,64]{2,1,0:T(8,128)S(1)}, s32[]{:T(128)}, bf16[16,4]{1,0:T(8,128)(2,1)}, ...), condition=%wide.region_15.16_spmd, body=%wide.region_14.15_spmd.sunk | while | flops 49162 | bytes 164035 | solution.py:52
  591.1 0.9 convert_add_fusion.5
  594.0 39.5 %psum.47 = f32[256]{0:T(256)} all-reduce(f32[256]{0:T(256)S(1)} %get-tuple-element.263), channel_id=1, replica_groups=mesh['ctx'=16,'exp'=8,'dp'=2] {'ctx'}, use_global_device_ids=true, to_apply=%region_30.31 | all-reduce | flops 256 | bytes 2048 | tf_op jit(solution)/shard_map/psum | solution.py:232
  636.8 45.7 %all-reduce.2 = (bf16[128,64]{0,1:T(8,128)(2,1)S(1)}, bf16[128,64]{0,1:T(8,128)(2,1)S(1)}) all-reduce(bf16[128,64]{0,1:T(8,128)(2,1)S(1)} %fusion.16, bf16[128,64]{0,1:T(8,128)(2,1)S(1)} %fusion.17), channel_id=1, replica_groups=mesh['ctx'=16,'exp'=8,'dp'=2] {'exp','dp'}, use_global_device_ids=true, to_apply=%region_17.18 | all-reduce | flops 16384 | bytes 65536 | tf_op jit(solution)/shard_map/psum | solution.py:239
  683.9 1.1 reduce_window_sum.47
  685.1 1.1 reduce_window_sum.48
  (152 shorter events, 40.6 us)
Async XLA Ops:
  7.2 270.6 %copy-start = (bf16[1,4096,256]{2,1,0:T(8,128)(2,1)S(1)}, bf16[1,4096,256]{2,1,0:T(8,128)(2,1)}, u32[]{:S(2)}) copy-start(bf16[1,4096,256]{2,1,0:T(8,128)(2,1)} %param.26) | copy-start | bytes 6291460
  7.2 59.6 %copy-start.11 = (bf16[128,64]{0,1:T(8,128)(2,1)S(1)}, bf16[128,64]{0,1:T(8,128)(2,1)}, u32[]{:S(2)}) copy-start(bf16[128,64]{0,1:T(8,128)(2,1)} %param.18) | copy-start | bytes 49156
  7.2 87.4 %copy-start.10 = (bf16[128,64]{0,1:T(8,128)(2,1)S(1)}, bf16[128,64]{0,1:T(8,128)(2,1)}, u32[]{:S(2)}) copy-start(bf16[128,64]{0,1:T(8,128)(2,1)} %param.19) | copy-start | bytes 49156
  7.2 89.4 %copy-start.14 = (bf16[128,256]{1,0:T(8,128)(2,1)S(1)}, bf16[128,256]{1,0:T(8,128)(2,1)}, u32[]{:S(2)}) copy-start(bf16[128,256]{1,0:T(8,128)(2,1)} %param.16) | copy-start | bytes 196612
  7.2 113.6 %copy-start.15 = (f32[256]{0:T(256)S(1)}, f32[256]{0:T(256)}, u32[]{:S(2)}) copy-start(f32[256]{0:T(256)} %param.23) | copy-start | bytes 3076
  7.2 247.8 %all-gather.6.cloned.1.call-start = ((), (), s32[]{:S(2)}) async-start(), calls=%async_computation.9 | async-start | bytes 5406720 | tf_op jit(solution)/shard_map/all_gather | solution.py:193
  43.6 337.8 %reduce-scatter.5.cloned.1.call-start = ((), (), s32[]{:S(2)}) async-start(), calls=%async_computation.8 | async-start | bytes 5406720 | tf_op jit(solution)/shard_map/reduce_scatter | solution.py:176
  66.4 67.9 %copy-start.17 = (f32[4,128]{1,0:T(4,128)}, f32[4,128]{1,0:T(4,128)S(1)}, u32[]{:S(2)}) copy-start(f32[4,128]{1,0:T(4,128)S(1)} %copy.152) | copy-start | bytes 6148
  94.8 39.5 %copy-start.12 = (f32[128,128]{1,0:T(8,128)}, f32[128,128]{1,0:T(8,128)S(1)}, u32[]{:S(2)}) copy-start(f32[128,128]{1,0:T(8,128)S(1)} %fusion.65) | copy-start | bytes 196612
  95.8 38.5 %copy-start.16 = (bf16[16,4]{1,0:T(8,128)(2,1)}, bf16[16,4]{1,0:T(8,128)(2,1)S(1)}, u32[]{:S(2)}) copy-start(bf16[16,4]{1,0:T(8,128)(2,1)S(1)} %get-tuple-element.433) | copy-start | bytes 388
  277.8 4.2 copy-start.3
  277.8 4.2 copy-start.20
  287.0 3.9 copy-start.7
  295.6 1.6 copy-start.2
  295.6 181.6 %reduce-scatter.3.cloned.1.call-start = ((), (), s32[]{:S(2)}) async-start(), calls=%async_computation.7 | async-start | bytes 5406720 | tf_op jit(solution)/shard_map/reduce_scatter | solution.py:203
  297.2 1.6 copy-start.4
  297.2 1.6 copy-start.5
  320.4 1.0 copy-start.8
  383.1 95.8 %all-to-all-start.4 = ((bf16[1,40,8,256]{3,1,0,2:T(8,128)(2,1)}), bf16[1,40,8,256]{3,1,0,2:T(8,128)(2,1)S(1)}, u32[]{:S(2)}, u32[]{:S(2)}) async-start(bf16[1,40,8,256]{3,1,0,2:T(8,128)(2,1)} %copy.179), calls=%async_computation.6 | async-start | bytes 327680 | tf_op jit(solution)/shard_map/all_to_all | solution.py:183
  390.1 96.0 %copy-start.6 = (bf16[640,256]{1,0:T(8,128)(2,1)S(1)}, bf16[640,256]{1,0:T(8,128)(2,1)}, u32[]{:S(2)}) copy-start(bf16[640,256]{1,0:T(8,128)(2,1)} %get-tuple-element.297) | copy-start | bytes 983044
  478.8 16.7 %all-to-all-start.3 = ((bf16[1,40,8,256]{3,1,0,2:T(8,128)(2,1)}), bf16[1,40,8,256]{3,1,0,2:T(8,128)(2,1)S(1)}, u32[]{:S(2)}, u32[]{:S(2)}) async-start(bf16[1,40,8,256]{3,1,0,2:T(8,128)(2,1)} %copy.171), calls=%async_computation.4 | async-start | bytes 327680 | tf_op jit(solution)/shard_map/all_to_all | solution.py:210
  486.1 58.1 %copy-start.9 = (bf16[128,256]{1,0:T(8,128)(2,1)S(1)}, bf16[128,256]{1,0:T(8,128)(2,1)}, u32[]{:S(2)}) copy-start(bf16[128,256]{1,0:T(8,128)(2,1)} %param.27) | copy-start | bytes 196612
  486.1 58.1 %copy-start.19 = (f32[128]{0:T(128)S(1)}, f32[128]{0:T(128)}, u32[]{:S(2)}) copy-start(f32[128]{0:T(128)} %get-tuple-element.300) | copy-start | bytes 1540
  491.8 142.3 %copy-start.13 = (f32[128,128]{1,0:T(8,128)S(1)}, f32[128,128]{1,0:T(8,128)}, u32[]{:S(2)}) copy-start(f32[128,128]{1,0:T(8,128)} %copy-done.12) | copy-start | bytes 196612
  491.8 142.3 %copy-start.18 = (f32[4,128]{1,0:T(4,128)S(1)}, f32[4,128]{1,0:T(4,128)}, u32[]{:S(2)}) copy-start(f32[4,128]{1,0:T(4,128)} %copy-done.17) | copy-start | bytes 6148
  495.5 191.3 %copy-start.1 = (bf16[1,4096,256]{2,1,0:T(8,128)(2,1)S(1)}, bf16[1,4096,256]{2,1,0:T(8,128)(2,1)}, u32[]{:S(2)}) copy-start(bf16[1,4096,256]{2,1,0:T(8,128)(2,1)} %param.26) | copy-start | bytes 6291460
Sparse Core Ops, SparseCore 0:
  43.7 49.1 all-gather.5
  295.7 85.6 reduce-scatter.4
  385.4 91.7 reduce-scatter.2
